TPU v7x, 32 devices: a whole 2x2x4 slice. The times are simulated.
32 devices in a mesh: occ: 4 (over y, core), aux: 8 (over z, x).
Axes of the slice: x: 2, y: 2, z: 4, core: 2. Of those that a mesh axis runs over, the one named last changes fastest.
Arguments:
- pair_ints: bfloat16 [16, 128, 20480], P(None, None, ('aux', 'occ')), may hold values from -110 to 110
- domain_len: int32 [4], replicated, may hold values from 1 to 4, as said below
- domain_blocks: int32 [4, 4], replicated, may hold values from 0 to 703
- slot_orbital: int32 [4], replicated, may hold values from 0 to 3, each once
- virt_energy: float32 [90112], replicated, may hold values from 0.1 to 3
- occ_energy: float32 [4], replicated, may hold values from -2 to -0.3
Outputs:
- projected: bfloat16 [4, 512, 20480], P('occ', None, 'aux')
Inputs may be any that keep to these rules, and one draw needn't show every extreme that they name: `domain_len`: some orbital has exactly 4 live blocks. `slot_orbital`: each orbital is owned by exactly one group.
All inputs are finite; a program needn't handle non-finite values.
Results may differ from a plain program's by a relative error of at most 0.001.
The roundings to bfloat16 on the way count: a program that leaves them out, or rounds other values in their place, can miss the bound.
Values may be sent and summed in bfloat16 or wider, within the bound.
A program may use at most 128 MiB of HBM per device.

v0:
```python
import jax
import jax.numpy as jnp
from jax import lax
from jax.sharding import PartitionSpec as P

LEVEL_RATIO = 0.5
EPSILON = 1e-05


def local(pair_ints, domain_len, domain_blocks, slot_orbital, virt_energy, occ_energy):
    orbitals = domain_len.shape[0]
    block_count = domain_blocks.shape[1]
    block_rows = pair_ints.shape[1]
    local_cols = pair_ints.shape[2]
    domain_size = block_count * block_rows
    slot_ids = jnp.arange(block_count, dtype=jnp.int32)
    ordered_len = jnp.take(domain_len, slot_orbital, axis=0)
    starts = (slot_orbital * block_count)[:, None] + slot_ids[None, :]
    live_mask = slot_ids[None, :] < ordered_len[:, None]
    flat_index = starts.reshape(-1)
    picked = jnp.take(pair_ints, flat_index, axis=0)
    picked = jnp.where(live_mask.reshape(-1)[:, None, None], picked, jnp.zeros_like(picked))
    padded = picked.reshape(orbitals, domain_size, local_cols)
    regrouped = lax.all_to_all(padded, "occ", split_axis=0, concat_axis=2, tiled=True)
    own_rows = regrouped[0]
    owner_group = lax.axis_index("occ")
    orbital = lax.dynamic_index_in_dim(slot_orbital, owner_group, 0, keepdims=False)
    partials = jnp.einsum("oac,obc->oab", padded, padded, preferred_element_type=jnp.float32)
    gram_part = lax.psum_scatter(
        partials.reshape(orbitals * domain_size, domain_size),
        ("occ", "aux"),
        scatter_dimension=0,
        tiled=True,
    )
    gram_sum = lax.all_gather(gram_part, "aux", axis=0, tiled=True)
    energy_table = virt_energy.reshape(-1, block_rows)
    blocks = lax.dynamic_index_in_dim(domain_blocks, orbital, 0, keepdims=False)
    energies = jnp.take(energy_table, blocks, axis=0).reshape(domain_size)
    occ_level = lax.dynamic_index_in_dim(occ_energy, orbital, 0, keepdims=False)
    denominator = energies[:, None] + energies[None, :] - 2.0 * occ_level
    amplitude = gram_sum / denominator
    length = lax.dynamic_index_in_dim(domain_len, orbital, 0, keepdims=False).astype(jnp.float32)
    level_shift = LEVEL_RATIO * (jnp.trace(amplitude) / (block_rows * length) + EPSILON)
    factor = jnp.linalg.cholesky(amplitude + level_shift * jnp.eye(domain_size, dtype=jnp.float32))
    solved = jax.scipy.linalg.cho_solve((factor, True), amplitude)
    projector = solved.T.astype(jnp.bfloat16)
    projected = jnp.dot(projector, own_rows, preferred_element_type=jnp.float32).astype(
        jnp.bfloat16
    )
    return projected[None]


def solution(mesh):
    placed = (P(None, None, ("aux", "occ")), P(), P(), P(), P(), P())
    return jax.shard_map(
        local, mesh=mesh, in_specs=placed, out_specs=P("occ", None, "aux"), check_vma=False
    )
```

profile of v0, /device:TPU:0, one launch (start us, length us, event | category | flops | bytes accessed | tf_op | source)
XLA Modules:
  0.0 390.7 jit_solution(3105162862275415704)
XLA Ops:
  6.5 0.8 compare_select_fusion.4
  7.4 1.3 gather_fusion
  8.6 0.7 and_select_fusion
  9.7 2.4 gather_fusion.1
  12.1 2.1 fusion.1
  14.2 3.8 fusion.62
  18.1 4.7 %all-to-all-start = ((bf16[4,512,640]{2,1,0:T(8,128)(2,1)}), bf16[4,512,640]{2,1,0:T(8,128)(2,1)}, u32[]{:S(2)}, u32[]{:S(2)}) async-start(bf16[4,512,640]{2,1,0:T(8,128)(2,1)} %copy-done.2), calls=%async_computation | async-start | bytes 5242880 | tf_op jit(solution)/shard_map/all_to_all | solution.py:24
  22.8 143.1 %reduce-scatter.4.cloned.1.call-done = f32[64,512]{1,0:T(8,128)} async-done(((f32[2048,512]{1,0:T(8,128)}), f32[64,512]{1,0:T(8,128)}) %reduce-scatter.4.cloned.1.call-update) | async-done | bytes 131088 | tf_op jit(solution)/shard_map/reduce_scatter | solution.py:29
  165.9 0.7 dynamic_slice.15
  168.7 0.7 dynamic_slice.18
  169.3 0.7 dynamic_slice.17
  170.7 1.5 gather_fusion.2
  173.1 4.8 %copy.58 = bf16[1,512,4,640]{1,3,2,0:T(8,128)(2,1)} copy(bf16[1,512,4,640]{3,1,2,0:T(8,128)(2,1)} %bitcast.23) | data formatting | bytes 5242880 | tf_op jit(solution)/shard_map/all_to_all | solution.py:24
  177.9 28.2 %all-gather.2.cloned.1.call-done = f32[512,512]{1,0:T(8,128)} async-done(((f32[64,512]{1,0:T(8,128)}), f32[512,512]{1,0:T(8,128)}) %all-gather.2.cloned.1.call-update) | async-done | bytes 1048592 | tf_op jit(solution)/shard_map/all_gather | solution.py:35
  206.2 2.6 copy.45
  208.8 3.2 select_reduce_fusion
  212.6 2.3 select_add_fusion
  215.0 2.5 copy.46
  217.5 1.8 fusion.2
  219.3 1.0 copy-done.5
  220.3 11.7 %cholesky.103 = f32[128,128]{1,0:T(8,128)S(1)} custom-call(f32[128,128]{1,0:T(8,128)S(1)} %cholesky.263), custom_call_target="Cholesky" | custom-call | tf_op jit(solution)/shard_map/jit(cholesky)/cholesky | solution.py:44
  232.0 9.8 %custom-call.34 = f32[1,128,128]{1,2,0:T(8,128)S(1)} custom-call(f32[1,128,128]{2,1,0:T(8,128)S(1)} %get-tuple-element.46), custom_call_target="InvertDiagBlocksLowerTriangular" | custom-call | tf_op jit(solution)/shard_map/jit(cholesky)/cholesky | solution.py:44
  241.9 1.2 fusion.32
  243.1 1.3 convolution_subtract_fusion.6
  244.4 11.7 %cholesky.215 = f32[128,128]{1,0:T(8,128)S(1)} custom-call(f32[128,128]{1,0:T(8,128)S(1)} %cholesky.267), custom_call_target="Cholesky" | custom-call | tf_op jit(solution)/shard_map/jit(cholesky)/cholesky | solution.py:44
  256.5 10.0 %custom-call.35 = f32[1,128,128]{1,2,0:T(8,128)S(1)} custom-call(f32[1,128,128]{2,1,0:T(8,128)S(1)} %get-tuple-element.44), custom_call_target="InvertDiagBlocksLowerTriangular" | custom-call | tf_op jit(solution)/shard_map/jit(cholesky)/cholesky | solution.py:44
  266.9 1.0 copy-done.3
  267.9 1.5 convolution_subtract_fusion.7
  269.4 11.7 %cholesky.236 = f32[128,128]{1,0:T(8,128)S(1)} custom-call(f32[128,128]{1,0:T(8,128)S(1)} %cholesky.272), custom_call_target="Cholesky" | custom-call | tf_op jit(solution)/shard_map/jit(cholesky)/cholesky | solution.py:44
  281.9 9.8 %custom-call.36 = f32[1,128,128]{1,2,0:T(8,128)S(1)} custom-call(f32[1,128,128]{2,1,0:T(8,128)S(1)} %get-tuple-element.42), custom_call_target="InvertDiagBlocksLowerTriangular" | custom-call | tf_op jit(solution)/shard_map/jit(cholesky)/cholesky | solution.py:44
  291.7 1.0 convolution_dynamic-update-slice_fusion.1
  292.7 1.6 convolution_subtract_fusion.8
  294.2 11.9 %cholesky.253 = f32[128,128]{1,0:T(8,128)S(1)} custom-call(f32[128,128]{1,0:T(8,128)S(1)} %convolution_subtract_fusion.8), custom_call_target="Cholesky" | custom-call | tf_op jit(solution)/shard_map/jit(cholesky)/cholesky | solution.py:44
  306.9 0.7 compare_reduce_fusion.3
  307.6 0.7 compare_reduce_fusion.1
  308.3 0.7 compare_reduce_fusion
  312.1 2.4 select_select_fusion
  314.5 14.2 %while.1 = (s32[]{:T(128)}, f32[512,512]{0,1:T(8,128)}, s32[4,2]{0,1:T(2,128)S(1)}, f32[4,128,128]{2,1,0:T(8,128)}, s32[]{:T(128)}) while((s32[]{:T(128)}, f32[512,512]{0,1:T(8,128)}, s32[4,2]{0,1:T(2,128)S(1)}, f32[4,128,128]{2,1,0:T(8,128)}, s32[]{:T(128)}) %tuple.32), condition=%wide.while_cond, body=%wide.while_body.sunk | while | flops 2 | bytes 393829 | solution.py:45
  315.1 2.2 dynamic-slice.7
  318.7 2.2 dynamic-slice.7
  322.2 2.2 dynamic-slice.7
  325.8 2.2 dynamic-slice.7
  328.7 40.1 %custom-call.37 = f32[4,128,128]{1,2,0:T(8,128)S(1)} custom-call(f32[4,128,128]{2,1,0:T(8,128)} %get-tuple-element.12), custom_call_target="InvertDiagBlocksLowerTriangular" | custom-call | tf_op jit(solution)/shard_map/jit(_cho_solve)/triangular_solve | solution.py:45
  368.8 1.5 fusion.26
  370.3 1.6 convolution_subtract_fusion.3
  372.3 2.0 convolution_subtract_fusion.2
  374.8 2.4 convolution_subtract_fusion.5
  380.6 3.1 fusion
  (85 shorter events, 13.2 us)
Async XLA Ops:
  6.5 3.2 copy-start
  6.5 159.3 %reduce-scatter.4.cloned.1.call-start = ((), (), s32[]{:S(2)}) async-start(), calls=%async_computation.3 | async-start | bytes 4325376 | tf_op jit(solution)/shard_map/reduce_scatter | solution.py:29
  14.2 3.8 copy-start.2
  18.0 147.9 %copy-start.7 = (s32[4]{0:T(128)S(1)}, s32[4]{0:T(128)}, u32[]{:S(2)}) copy-start(s32[4]{0:T(128)} %param.9) | copy-start | bytes 52
  18.0 150.6 %copy-start.1 = (s32[4]{0:T(128)S(1)}, s32[4]{0:T(128)}, u32[]{:S(2)}) copy-start(s32[4]{0:T(128)} %param.7) | copy-start | bytes 52
  18.0 151.3 %copy-start.9 = (f32[4]{0:T(128)S(1)}, f32[4]{0:T(128)}, u32[]{:S(2)}) copy-start(f32[4]{0:T(128)} %param.11) | copy-start | bytes 52
  18.0 152.6 %copy-start.8 = (s32[4,4]{1,0:T(4,128)S(1)}, s32[4,4]{1,0:T(4,128)}, u32[]{:S(2)}) copy-start(s32[4,4]{1,0:T(4,128)} %param.8) | copy-start | bytes 196
  18.1 155.0 %all-to-all-start = ((bf16[4,512,640]{2,1,0:T(8,128)(2,1)}), bf16[4,512,640]{2,1,0:T(8,128)(2,1)}, u32[]{:S(2)}, u32[]{:S(2)}) async-start(bf16[4,512,640]{2,1,0:T(8,128)(2,1)} %copy-done.2), calls=%async_computation | async-start | bytes 5242880 | tf_op jit(solution)/shard_map/all_to_all | solution.py:24
  22.8 183.4 %all-gather.2.cloned.1.call-start = ((), (), s32[]{:S(2)}) async-start(), calls=%async_computation.2 | async-start | bytes 1179648 | tf_op jit(solution)/shard_map/all_gather | solution.py:35
  219.3 1.0 copy-start.5
  266.9 1.0 copy-start.3
  368.8 5.9 %copy-start.4 = (f32[512,512]{0,1:T(8,128)S(1)}, f32[512,512]{0,1:T(8,128)}, u32[]{:S(2)}) copy-start(f32[512,512]{0,1:T(8,128)} %get-tuple-element.107) | copy-start | bytes 3145732
  378.0 2.6 copy-start.6
Sparse Core Ops, SparseCore 0:
  18.1 147.6 reduce-scatter.3
  168.0 38.1 all-gather.1
where the time goes:
time: 394 us; the launch traced here: 391 us
  waiting for transfers between devices  171 us (43%)
  other arithmetic  133 us (34%)
  local copies, waits for them, and re-layouts  35.5 us (9%)
  matrix products  25.2 us (6%)
  between operations  20.8 us (5%)
  starting transfers between devices  4.74 us (1%)
    reduce_scatter x1, waiting for transfers between devices, local(): lax.psum_scatter(partials.reshape(orbitals * domain_size, domain_size), (...  143 us
    another operation x15, other arithmetic, local(): jnp.linalg.cholesky(amplitude + level_shift * jnp.eye(domain_size, dtype=...  79.4 us
    another operation x3, other arithmetic, local(): solved = jax.scipy.linalg.cho_solve((factor, True), amplitude)  42.5 us
    all_gather x1, waiting for transfers between devices, local(): gram_sum = lax.all_gather(gram_part, 'aux', axis=0, tiled=True)  28.2 us
    another operation x20, local copies, waits for them, and re-layouts  14.2 us
    another operation x14, matrix products, local(): solved = jax.scipy.linalg.cho_solve((factor, True), amplitude)  11.6 us
  transfers between devices with their start and end apart: 3, of which 2 were waited for; matrix products, arithmetic and copies ran while one was open for 2% of the time, Pallas kernels for 0%

commit v1 on v0

--- a/solution.py
+++ b/solution.py
@@ -5,6 +5,24 @@
 
 LEVEL_RATIO = 0.5
 EPSILON = 1e-05
+
+
+def laid_out(blocks, dim):
+    shape = list(blocks.shape[1:])
+    shape[dim] *= blocks.shape[0]
+    return jnp.moveaxis(blocks, 0, dim).reshape(shape)
+
+
+def collected_by_bits(value, axis):
+    peers = lax.axis_size(axis)
+    parts = value[None]
+    for level in range(peers.bit_length() - 1):
+        bit = 1 << level
+        received = lax.ppermute(parts, axis, [(i, i ^ bit) for i in range(peers)])
+        both = jnp.stack([parts, received])
+        upper = lax.axis_index(axis) >> level & 1
+        parts = jnp.where(upper == 0, both, both[::-1]).reshape(-1, *value.shape)
+    return parts
 
 
 def local(pair_ints, domain_len, domain_blocks, slot_orbital, virt_energy, occ_energy):
@@ -32,7 +50,7 @@
         scatter_dimension=0,
         tiled=True,
     )
-    gram_sum = lax.all_gather(gram_part, "aux", axis=0, tiled=True)
+    gram_sum = laid_out(collected_by_bits(gram_part, "aux"), 0)
     energy_table = virt_energy.reshape(-1, block_rows)
     blocks = lax.dynamic_index_in_dim(domain_blocks, orbital, 0, keepdims=False)
     energies = jnp.take(energy_table, blocks, axis=0).reshape(domain_size)

time: 394 us -> 390 us (0.990)
  waiting for transfers between devices: 171 us -> 164 us
    all_gather x1 -> x0, waiting for transfers between devices: 28.2 us -> none  [local(): gram_sum = lax.all_gather(gram_part, 'aux', axis=0, tiled=True)]
    ppermute x0 -> x3, waiting for transfers between devices: none -> 23.7 us  [collected_by_bits(): received = lax.ppermute(parts, axis, [(i, i ^ bit) for i in range(peers)])]
    another operation x20 -> x21, local copies, waits for them, and re-layouts: 14.2 us -> 16.8 us
  transfers between devices with their start and end apart: 3 -> 5, of which waited for: 2 -> 4; matrix products, arithmetic and copies ran while one was open for 2% -> 3% of each run, Pallas kernels for 0% -> 0%
where the time goes in v1:
time: 390 us; the launch traced here: 385 us
  waiting for transfers between devices  164 us (42%)
  other arithmetic  135 us (35%)
  local copies, waits for them, and re-layouts  36 us (9%)
  matrix products  25.2 us (6%)
  between operations  20.4 us (5%)
  starting transfers between devices  4.84 us (1%)
    reduce_scatter x1, waiting for transfers between devices, local(): lax.psum_scatter(partials.reshape(orbitals * domain_size, domain_size), (...  141 us
    another operation x15, other arithmetic, local(): jnp.linalg.cholesky(amplitude + level_shift * jnp.eye(domain_size, dtype=...  79.3 us
    another operation x3, other arithmetic, local(): solved = jax.scipy.linalg.cho_solve((factor, True), amplitude)  42.5 us
    ppermute x3, waiting for transfers between devices, collected_by_bits(): received = lax.ppermute(parts, axis, [(i, i ^ bit) for i in range(peers)])  23.7 us
    another operation x20, local copies, waits for them, and re-layouts  14.2 us
    another operation x14, matrix products, local(): solved = jax.scipy.linalg.cho_solve((factor, True), amplitude)  11.6 us
  transfers between devices with their start and end apart: 5, of which 4 were waited for; matrix products, arithmetic and copies ran while one was open for 3% of the time, Pallas kernels for 0%

profile of v1, /device:TPU:0, one launch (start us, length us, event | category | flops | bytes accessed | tf_op | source)
XLA Modules:
  0.0 385.5 jit_solution(2978926060407947458)
XLA Ops:
  6.5 0.8 compare_select_fusion.5
  7.4 1.3 gather_fusion
  9.7 2.4 gather_fusion.1
  12.1 2.1 fusion.1
  14.2 3.8 fusion.65
  18.1 4.7 %all-to-all-start = ((bf16[4,512,640]{2,1,0:T(8,128)(2,1)}), bf16[4,512,640]{2,1,0:T(8,128)(2,1)}, u32[]{:S(2)}, u32[]{:S(2)}) async-start(bf16[4,512,640]{2,1,0:T(8,128)(2,1)} %copy-done.2), calls=%async_computation.1 | async-start | bytes 5242880 | tf_op jit(solution)/shard_map/all_to_all | solution.py:42
  25.3 140.7 %reduce-scatter.2.cloned.1.call-done = f32[64,512]{1,0:T(8,128)} async-done(((f32[2048,512]{1,0:T(8,128)}), f32[64,512]{1,0:T(8,128)}) %reduce-scatter.2.cloned.1.call-update) | async-done | bytes 131088 | tf_op jit(solution)/shard_map/reduce_scatter | solution.py:47
  166.1 5.1 %collective-permute-done = f32[1,64,512]{2,1,0:T(8,128)S(1)} collective-permute-done((f32[1,64,512]{2,1,0:T(8,128)}, f32[1,64,512]{2,1,0:T(8,128)S(1)}, u32[]{:S(2)}, u32[]{:S(2)}) %collective-permute-start) | collective-permute-done | bytes 131104 | tf_op jit(solution)/shard_map/ppermute | solution.py:21
  171.3 0.9 pad_maximum_fusion.2
  172.4 0.7 dynamic_slice.18
  173.0 1.5 gather_fusion.2
  176.8 3.6 collective-permute-done.1
  180.7 4.8 %copy.43 = bf16[1,512,4,640]{1,3,2,0:T(8,128)(2,1)} copy(bf16[1,512,4,640]{3,1,2,0:T(8,128)(2,1)} %bitcast.33) | data formatting | bytes 5242880 | tf_op jit(solution)/shard_map/all_to_all | solution.py:42
  185.5 15.0 %collective-permute-done.2 = f32[4,64,512]{2,1,0:T(8,128)} collective-permute-done((f32[4,64,512]{2,1,0:T(8,128)S(1)}, f32[4,64,512]{2,1,0:T(8,128)}, u32[]{:S(2)}, u32[]{:S(2)}) %collective-permute-start.2) | collective-permute-done | bytes 524320 | tf_op jit(solution)/shard_map/ppermute | solution.py:21
  200.5 1.1 pad_maximum_fusion
  201.6 2.0 select_reduce_fusion
  203.6 2.6 copy.30
  206.8 2.8 select_add_fusion
  209.6 2.5 copy.31
  212.1 1.8 fusion.2
  213.9 1.0 copy-done.5
  215.0 11.7 %cholesky.103 = f32[128,128]{1,0:T(8,128)S(1)} custom-call(f32[128,128]{1,0:T(8,128)S(1)} %cholesky.263), custom_call_target="Cholesky" | custom-call | tf_op jit(solution)/shard_map/jit(cholesky)/cholesky | solution.py:62
  226.7 9.8 %custom-call.34 = f32[1,128,128]{1,2,0:T(8,128)S(1)} custom-call(f32[1,128,128]{2,1,0:T(8,128)S(1)} %get-tuple-element.46), custom_call_target="InvertDiagBlocksLowerTriangular" | custom-call | tf_op jit(solution)/shard_map/jit(cholesky)/cholesky | solution.py:62
  236.5 1.2 fusion.34
  237.8 1.3 convolution_subtract_fusion.6
  239.0 11.7 %cholesky.215 = f32[128,128]{1,0:T(8,128)S(1)} custom-call(f32[128,128]{1,0:T(8,128)S(1)} %cholesky.267), custom_call_target="Cholesky" | custom-call | tf_op jit(solution)/shard_map/jit(cholesky)/cholesky | solution.py:62
  251.3 9.8 %custom-call.35 = f32[1,128,128]{1,2,0:T(8,128)S(1)} custom-call(f32[1,128,128]{2,1,0:T(8,128)S(1)} %get-tuple-element.44), custom_call_target="InvertDiagBlocksLowerTriangular" | custom-call | tf_op jit(solution)/shard_map/jit(cholesky)/cholesky | solution.py:62
  261.6 1.0 copy-done.3
  262.6 1.5 convolution_subtract_fusion.7
  264.1 11.7 %cholesky.236 = f32[128,128]{1,0:T(8,128)S(1)} custom-call(f32[128,128]{1,0:T(8,128)S(1)} %cholesky.272), custom_call_target="Cholesky" | custom-call | tf_op jit(solution)/shard_map/jit(cholesky)/cholesky | solution.py:62
  276.6 9.8 %custom-call.36 = f32[1,128,128]{1,2,0:T(8,128)S(1)} custom-call(f32[1,128,128]{2,1,0:T(8,128)S(1)} %get-tuple-element.42), custom_call_target="InvertDiagBlocksLowerTriangular" | custom-call | tf_op jit(solution)/shard_map/jit(cholesky)/cholesky | solution.py:62
  286.4 0.9 convolution_dynamic-update-slice_fusion.1
  287.4 1.6 convolution_subtract_fusion.8
  288.9 11.9 %cholesky.253 = f32[128,128]{1,0:T(8,128)S(1)} custom-call(f32[128,128]{1,0:T(8,128)S(1)} %convolution_subtract_fusion.8), custom_call_target="Cholesky" | custom-call | tf_op jit(solution)/shard_map/jit(cholesky)/cholesky | solution.py:62
  301.6 0.7 compare_reduce_fusion.3
  303.0 0.7 compare_reduce_fusion
  306.8 2.4 select_select_fusion
  309.2 14.2 %while.1 = (s32[]{:T(128)}, f32[512,512]{0,1:T(8,128)}, s32[4,2]{0,1:T(2,128)S(1)}, f32[4,128,128]{2,1,0:T(8,128)}, s32[]{:T(128)}) while((s32[]{:T(128)}, f32[512,512]{0,1:T(8,128)}, s32[4,2]{0,1:T(2,128)S(1)}, f32[4,128,128]{2,1,0:T(8,128)}, s32[]{:T(128)}) %tuple.33), condition=%wide.while_cond, body=%wide.while_body.sunk | while | flops 2 | bytes 393829 | solution.py:63
  309.8 2.2 dynamic-slice.7
  313.4 2.2 dynamic-slice.7
  317.0 2.2 dynamic-slice.7
  320.6 2.2 dynamic-slice.7
  323.4 40.1 %custom-call.37 = f32[4,128,128]{1,2,0:T(8,128)S(1)} custom-call(f32[4,128,128]{2,1,0:T(8,128)} %get-tuple-element.12), custom_call_target="InvertDiagBlocksLowerTriangular" | custom-call | tf_op jit(solution)/shard_map/jit(_cho_solve)/triangular_solve | solution.py:63
  363.6 1.5 fusion.26
  365.0 1.6 convolution_subtract_fusion.3
  367.1 2.0 convolution_subtract_fusion.2
  369.5 2.4 convolution_subtract_fusion.5
  375.3 3.1 fusion
  (101 shorter events, 16.6 us)
Async XLA Ops:
  6.5 3.2 copy-start
  6.5 159.5 %reduce-scatter.2.cloned.1.call-start = ((), (), s32[]{:S(2)}) async-start(), calls=%async_computation.2 | async-start | bytes 4325376 | tf_op jit(solution)/shard_map/reduce_scatter | solution.py:47
  14.2 3.8 copy-start.2
  18.0 4.8 %copy-start.7 = (s32[4]{0:T(128)S(1)}, s32[4]{0:T(128)}, u32[]{:S(2)}) copy-start(s32[4]{0:T(128)} %param.9) | copy-start | bytes 52
  18.0 7.2 %copy-start.8 = (s32[4,4]{1,0:T(4,128)S(1)}, s32[4,4]{1,0:T(4,128)}, u32[]{:S(2)}) copy-start(s32[4,4]{1,0:T(4,128)} %param.8) | copy-start | bytes 196
  18.0 154.3 %copy-start.1 = (s32[4]{0:T(128)S(1)}, s32[4]{0:T(128)}, u32[]{:S(2)}) copy-start(s32[4]{0:T(128)} %param.7) | copy-start | bytes 52
  18.0 156.8 %copy-start.9 = (f32[4]{0:T(128)S(1)}, f32[4]{0:T(128)}, u32[]{:S(2)}) copy-start(f32[4]{0:T(128)} %param.11) | copy-start | bytes 52
  18.1 162.6 %all-to-all-start = ((bf16[4,512,640]{2,1,0:T(8,128)(2,1)}), bf16[4,512,640]{2,1,0:T(8,128)(2,1)}, u32[]{:S(2)}, u32[]{:S(2)}) async-start(bf16[4,512,640]{2,1,0:T(8,128)(2,1)} %copy-done.2), calls=%async_computation.1 | async-start | bytes 5242880 | tf_op jit(solution)/shard_map/all_to_all | solution.py:42
  166.1 5.2 %collective-permute-start = (f32[1,64,512]{2,1,0:T(8,128)}, f32[1,64,512]{2,1,0:T(8,128)S(1)}, u32[]{:S(2)}, u32[]{:S(2)}) collective-permute-start(f32[1,64,512]{2,1,0:T(8,128)} %bitcast.119), channel_id=1, source_target_pairs={{0,1},{1,0},{2,3},{3,2},{4,5},{5,4},{6,7},{7,6},{8,9},{9,8},{10,11... | collective-permute-start | bytes 393224 | tf_op jit(solution)/shard_map/ppermute | solution.py:21
  172.3 8.1 %collective-permute-start.1 = (f32[2,64,512]{2,1,0:T(8,128)S(1)}, f32[2,64,512]{2,1,0:T(8,128)S(1)}, u32[]{:S(2)}, u32[]{:S(2)}) collective-permute-start(f32[2,64,512]{2,1,0:T(8,128)S(1)} %get-tuple-element.40), channel_id=1, source_target_pairs={{0,2},{1,3},{2,0},{3,1},{4,6},{5,7},{6,4},{7,5},{8,10},{9,11},{10,... | collective-permute-start | bytes 786440 | tf_op jit(solution)/shard_map/ppermute | solution.py:21
  180.5 20.0 %collective-permute-start.2 = (f32[4,64,512]{2,1,0:T(8,128)S(1)}, f32[4,64,512]{2,1,0:T(8,128)}, u32[]{:S(2)}, u32[]{:S(2)}) collective-permute-start(f32[4,64,512]{2,1,0:T(8,128)S(1)} %bitcast.116), channel_id=1, source_target_pairs={{0,4},{1,5},{2,6},{3,7},{4,0},{5,1},{6,2},{7,3},{8,12},{9,13},{10,... | collective-permute-start | bytes 1572872 | tf_op jit(solution)/shard_map/ppermute | solution.py:21
  213.9 1.0 copy-start.5
  261.6 1.0 copy-start.3
  363.6 5.9 %copy-start.4 = (f32[512,512]{0,1:T(8,128)S(1)}, f32[512,512]{0,1:T(8,128)}, u32[]{:S(2)}) copy-start(f32[512,512]{0,1:T(8,128)} %get-tuple-element.106) | copy-start | bytes 3145732
  372.7 2.6 copy-start.6
Sparse Core Ops, SparseCore 0:
  18.1 147.9 reduce-scatter.1
